TPU v7x, 32 devices: a whole 2x2x4 slice. The times are simulated.
32 devices in a mesh: row: 8 (over y, x, core), col: 4 (over z).
Axes of the slice: x: 2, y: 2, z: 4, core: 2. Of those that a mesh axis runs over, the one named last changes fastest.
Arguments:
- amplitudes: bfloat16 [2048, 8192], P('row', 'col'), may hold values from -0.125 to 0.125
- integrals: bfloat16 [8192, 1024], P('col', 'row'), may hold values from -6 to 6
- occ_irrep: int32 [200], replicated, may hold values from 0 to 3
- vir_irrep: int32 [6], replicated, may hold values from 0 to 3
- occ_energy: float32 [200], replicated, may hold values from -1 to -0.3
- vir_energy: float32 [1536], replicated, may hold values from 0.2 to 1.5
Outputs:
- update: float32 [2048, 1024], P('row', 'col')
All inputs are finite; a program needn't handle non-finite values.
Results may differ from a plain program's by a relative error of at most 0.0003.
Values may be sent and summed in bfloat16 or wider, within the bound.
A program may use at most 128 MiB of HBM per device.

v0:
```python
import jax
import jax.numpy as jnp
from jax import lax
from jax.sharding import PartitionSpec as P

TILE = 256


def lookup(table, index):
    hits = index[:, None] == jnp.arange(table.shape[0], dtype=jnp.int32)[None, :]
    return jnp.sum(jnp.where(hits, table[None, :], jnp.zeros_like(table)[None, :]), axis=1)


def irreps(first_tile, count, occ_irrep, vir_irrep, tiles_virtual):
    tiles = first_tile + jnp.arange(count, dtype=jnp.int32)
    return jnp.bitwise_xor(
        lookup(occ_irrep, tiles // tiles_virtual), lookup(vir_irrep, tiles % tiles_virtual)
    )


def shards(amplitudes, integrals, occ_irrep, vir_irrep, occ_energy, vir_energy):
    tile_size = TILE
    tiles_virtual = vir_irrep.shape[0]
    virtual_count = vir_energy.shape[0]
    p_rows, k_cols = amplitudes.shape
    p_tiles = p_rows // tile_size
    k_tiles = k_cols // tile_size
    row_index = lax.axis_index("row")
    col_index = lax.axis_index("col")
    p_irr = irreps(row_index * p_tiles, p_tiles, occ_irrep, vir_irrep, tiles_virtual)
    k_irr = irreps(col_index * k_tiles, k_tiles, occ_irrep, vir_irrep, tiles_virtual)
    match = p_irr[:, None] == k_irr[None, :]
    masked_amp = (
        amplitudes.reshape(p_tiles, tile_size, k_tiles, tile_size)
        * match[:, None, :, None].astype(jnp.bfloat16)
    ).reshape(p_rows, k_cols)
    piece = lax.all_gather(integrals, "row", axis=1, tiled=True)
    width = piece.shape[1]
    columns = jnp.arange(width, dtype=jnp.int32)
    column_tiles = columns // tile_size
    q_irr = jnp.bitwise_xor(
        lookup(occ_irrep, column_tiles // tiles_virtual),
        lookup(vir_irrep, column_tiles % tiles_virtual),
    )
    keeper = (k_irr[:, None] == q_irr[None, :]).astype(jnp.bfloat16)
    masked_int = (piece.reshape(k_tiles, tile_size, width) * keeper[:, None, :]).reshape(
        k_cols, width
    )
    partial_cycle = jnp.dot(masked_amp, masked_int, preferred_element_type=jnp.float32)
    cycle = lax.psum_scatter(partial_cycle, "col", scatter_dimension=1, tiled=True)
    q_cols = cycle.shape[1]
    row_pairs = row_index * p_rows + jnp.arange(p_rows, dtype=jnp.int32)
    col_pairs = col_index * q_cols + jnp.arange(q_cols, dtype=jnp.int32)
    row_energy = lookup(vir_energy, row_pairs % virtual_count) - lookup(
        occ_energy, row_pairs // virtual_count
    )
    col_energy = lookup(vir_energy, col_pairs % virtual_count) - lookup(
        occ_energy, col_pairs // virtual_count
    )
    return cycle / (row_energy[:, None] + col_energy[None, :])


def solution(mesh):
    return jax.shard_map(
        shards,
        mesh=mesh,
        in_specs=(P("row", "col"), P("col", "row"), P(), P(), P(), P()),
        out_specs=P("row", "col"),
        check_vma=False,
    )
```

profile of v0, /device:TPU:6, one launch (start us, length us, event | category | flops | bytes accessed | tf_op | source)
XLA Modules:
  0.0 88.6 jit_solution(15348805814109380843)
XLA Ops:
  6.5 0.0 all-gather.2.cloned.1.call-start
  6.5 0.7 all-gather.2.cloned.1.call-update
  7.3 0.0 reduce-scatter.2.cloned.1.call-start
  7.3 1.3 %fusion.19 = s32[]{:T(128)} fusion(s32[6]{0:T(128)} %param.9, s32[]{:T(128)} %bitcast.4), kind=kLoop, calls=%fused_computation.56 | loop fusion | flops 17 | bytes 32 | tf_op jit(solution)/shard_map/reduce_sum | solution.py:11
  8.7 1.3 %fusion.14 = s32[]{:T(128)} fusion(s32[200]{0:T(256)} %param.8, s32[]{:T(128)} %bitcast.3), kind=kLoop, calls=%fused_computation.49 | loop fusion | flops 599 | bytes 808 | tf_op jit(solution)/shard_map/reduce_sum | solution.py:11
  11.2 0.8 select_reduce_fusion.7
  12.1 0.9 select_reduce_fusion.6
  12.9 0.1 broadcast_bitcast_fusion
  13.1 0.7 select_reduce_fusion.5
  13.8 0.9 select_reduce_fusion.2
  14.7 0.1 compare_convert_fusion
  14.8 32.2 %all-gather.2.cloned.1.call-done = bf16[2048,1024]{1,0:T(8,128)(2,1)} async-done(((bf16[2048,128]{1,0:T(8,128)(2,1)}), bf16[2048,1024]{1,0:T(8,128)(2,1)}) %all-gather.2.cloned.1.call-update) | async-done | bytes 4194320 | tf_op jit(solution)/shard_map/all_gather | solution.py:37
  47.0 2.5 %bitcast_multiply_fusion = bf16[2048,1024]{1,0:T(8,128)(2,1)S(1)} fusion(bf16[2048,1024]{1,0:T(8,128)(2,1)} %all-gather.2.cloned.1.call-done, bf16[8,1024]{1,0:T(8,128)(2,1)S(1)} %compare_convert_fusion), kind=kLoop, calls=%fused_computation | loop fusion | flops 2097152 | bytes 8404992 | tf_op jit(solution)/shard_map/mul | solution.py:46
  49.4 0.0 copy-done.2
  49.4 0.0 copy-start.1
  49.5 0.0 copy-start
  49.5 2.3 %fusion = f32[256,1024]{1,0:T(8,128)} fusion(bf16[2048,1024]{1,0:T(8,128)(2,1)S(1)} %bitcast_multiply_fusion, bf16[256,2048]{1,0:T(8,128)(2,1)S(1)} %copy-done.2, bf16[2048]{0:T(1024)(128)(2,1)S(1)} %bitcast.11), kind=kOutput, calls=%fused_computation.5 | convolution fusion | flops 1074266112 | bytes 6295552 | tf_op jit(solution)/shard_map/dot_general | solution.py:49
  51.7 0.0 reduce-scatter.2.cloned.1.call-update
  51.8 0.0 copy-done.1
  51.8 0.1 select_reduce_fusion.4
  52.0 0.0 copy-done
  52.0 0.5 select_reduce_fusion.1
  52.5 27.5 %reduce-scatter.2.cloned.1.call-done = f32[256,256]{1,0:T(8,128)} async-done(((f32[256,1024]{1,0:T(8,128)}), f32[256,256]{1,0:T(8,128)}) %reduce-scatter.2.cloned.1.call-update) | async-done | bytes 262160 | tf_op jit(solution)/shard_map/reduce_scatter | solution.py:50
  80.0 1.8 %add_divide_fusion = f32[256,256]{1,0:T(8,128)} fusion(f32[256,256]{1,0:T(8,128)} %reduce-scatter.2.cloned.1.call-done, f32[256]{0:T(256)S(1)} %sub.51, f32[256]{0:T(256)S(1)} %sub.49), kind=kLoop, calls=%fused_computation.10 | loop fusion | flops 131072 | bytes 526336 | tf_op jit(solution)/shard_map/div | solution.py:60
  (11 shorter events, 0.1 us)
Async XLA Ops:
  6.5 40.4 %all-gather.2.cloned.1.call-start = ((), (), s32[]{:S(2)}) async-start(), calls=%async_computation.1 | async-start | bytes 4718592 | tf_op jit(solution)/shard_map/all_gather | solution.py:37
  7.3 72.7 %reduce-scatter.2.cloned.1.call-start = ((), (), s32[]{:S(2)}) async-start(), calls=%async_computation.2 | async-start | bytes 1310720 | tf_op jit(solution)/shard_map/reduce_scatter | solution.py:50
  14.8 34.7 %copy-start.2 = (bf16[256,2048]{1,0:T(8,128)(2,1)S(1)}, bf16[256,2048]{1,0:T(8,128)(2,1)}, u32[]{:S(2)}) copy-start(bf16[256,2048]{1,0:T(8,128)(2,1)} %param.6) | copy-start | bytes 3145732
  49.4 2.4 %copy-start.1 = (f32[200]{0:T(256)S(1)}, f32[200]{0:T(256)}, u32[]{:S(2)}) copy-start(f32[200]{0:T(256)} %param.10) | copy-start | bytes 2404
  49.5 2.5 %copy-start = (f32[1536]{0:T(1024)S(1)}, f32[1536]{0:T(1024)}, u32[]{:S(2)}) copy-start(f32[1536]{0:T(1024)} %param.11) | copy-start | bytes 18436
Sparse Core Ops, SparseCore 0:
  9.2 37.6 all-gather.1
  51.9 28.0 reduce-scatter.1
where the time goes:
time: 90.4 us; the launch traced here: 88.6 us
  waiting for transfers between devices  60.4 us (67%)
  between operations  14.8 us (16%)
  other arithmetic  11 us (12%)
  matrix products  2.27 us (3%)
    all_gather x1, waiting for transfers between devices, shards(): piece = lax.all_gather(integrals, 'row', axis=1, tiled=True)  32.2 us
    reduce_scatter x1, waiting for transfers between devices, shards(): lax.psum_scatter(partial_cycle, 'col', scatter_dimension=1, tiled=True)  27.5 us
    reduce_sum x8, other arithmetic, lookup(): jnp.sum(jnp.where(hits, table[None, :], jnp.zeros_like(table)[None, :]),...  6.58 us
    mul x1, other arithmetic, shards(): piece.reshape(k_tiles, tile_size, width) * keeper[:, None, :]  2.47 us
    dot_general x1, matrix products, shards(): jnp.dot(masked_amp, masked_int, preferred_element_type=jnp.float32)  2.27 us
  transfers between devices with their start and end apart: 2, of which 2 were waited for; matrix products, arithmetic and copies ran while one was open for 8% of the time, Pallas kernels for 0%

commit v1 on v0

--- a/solution.py
+++ b/solution.py
@@ -1,9 +1,14 @@
+import functools
+
 import jax
 import jax.numpy as jnp
 from jax import lax
+from jax.experimental import pallas as pl
+from jax.experimental.pallas import tpu as pltpu
 from jax.sharding import PartitionSpec as P
 
 TILE = 256
+MESH = pl.DeviceIdType.MESH
 
 
 def lookup(table, index):
@@ -18,7 +23,7 @@
     )
 
 
-def shards(amplitudes, integrals, occ_irrep, vir_irrep, occ_energy, vir_energy):
+def general(amplitudes, integrals, occ_irrep, vir_irrep, occ_energy, vir_energy):
     tile_size = TILE
     tiles_virtual = vir_irrep.shape[0]
     virtual_count = vir_energy.shape[0]
@@ -60,7 +65,326 @@
     return cycle / (row_energy[:, None] + col_energy[None, :])
 
 
+CHUNKS = 4
+SPLITS = 2
+COLS = 128
+
+
+def cycle_kernel(
+    nz,
+    amp_hbm,
+    int_hbm,
+    occ_irr,
+    vir_irr,
+    occ_e,
+    vir_e,
+    out_ref,
+    blocks,
+    amp,
+    part,
+    incoming,
+    denom,
+    local_sem,
+    near_send,
+    near_recv,
+    fwd_send,
+    sib_send,
+    sib_recv,
+    z_send,
+    z_recv,
+):
+    r = lax.axis_index("row")
+    z = lax.axis_index("col")
+    core = r % 2
+    x = (r // 2) % 2
+    y = r // 4
+    xr = r + 2 - 4 * x
+    yr = r + 4 - 8 * y
+    dr = xr + yr - r
+    shift = 1 - 2 * core
+    sr = r + shift
+    rows_of = (r, xr, yr, dr)
+    depth = int_hbm.shape[0]
+    step = depth // CHUNKS
+    height = TILE // SPLITS
+    tiles_virtual = vir_irr.shape[0]
+    k_tiles = depth // TILE
+
+    int_copy = pltpu.make_async_copy(int_hbm, blocks.at[r], local_sem.at[0])
+    int_copy.start()
+    amp_copy = pltpu.make_async_copy(amp_hbm, amp, local_sem.at[1])
+    amp_copy.start()
+
+    barrier = pltpu.get_barrier_semaphore()
+    for target in (xr, yr, sr):
+        pl.semaphore_signal(barrier, inc=1, device_id=(target, z), device_id_type=MESH)
+
+    @pl.when(z > 0)
+    def _():
+        pl.semaphore_signal(barrier, inc=1, device_id=(r, z - 1), device_id_type=MESH)
+
+    @pl.when(z < nz - 1)
+    def _():
+        pl.semaphore_signal(barrier, inc=1, device_id=(r, z + 1), device_id_type=MESH)
+
+    ends = jnp.where(z > 0, 1, 0) + jnp.where(z < nz - 1, 1, 0)
+    pl.semaphore_wait(barrier, 3 + ends)
+
+    def at(ref, chunk):
+        return ref.at[pl.ds(chunk * step, step)]
+
+    def remote(src, dst, send_sem, recv_sem, target):
+        return pltpu.make_async_remote_copy(
+            src_ref=src,
+            dst_ref=dst,
+            send_sem=send_sem,
+            recv_sem=recv_sem,
+            device_id=target,
+            device_id_type=MESH,
+        )
+
+    half = CHUNKS // 2
+    x_order = list(range(CHUNKS))
+    y_order = x_order[half:] + x_order[:half]
+
+    def near(axis, chunk):
+        return remote(
+            at(int_hbm, chunk),
+            at(blocks.at[r], chunk),
+            near_send.at[axis, chunk],
+            near_recv.at[axis, chunk],
+            ((xr, yr)[axis], z),
+        )
+
+    def arrival(rel, chunk):
+        ref = at(blocks.at[rows_of[rel]], chunk)
+        return remote(ref, ref, near_send.at[0, chunk], near_recv.at[rel - 1, chunk], (xr, z))
+
+    def forward(chunk):
+        source, target = (xr, yr) if chunk < half else (yr, xr)
+        ref = at(blocks.at[source], chunk)
+        return remote(ref, ref, fwd_send.at[chunk], near_recv.at[2, chunk], (target, z))
+
+    def to_sibling(rel, chunk):
+        source = rows_of[rel]
+        src = at(int_hbm, chunk) if rel == 0 else at(blocks.at[source], chunk)
+        return remote(
+            src,
+            at(blocks.at[source], chunk),
+            sib_send.at[rel, chunk],
+            sib_recv.at[rel, chunk],
+            (sr, z),
+        )
+
+    def sibling_arrival(rel, chunk):
+        ref = at(blocks.at[rows_of[rel] + shift], chunk)
+        return remote(ref, ref, sib_send.at[rel, chunk], sib_recv.at[rel, chunk], (sr, z))
+
+    for cx, cy in zip(x_order, y_order):
+        near(0, cx).start()
+        near(1, cy).start()
+    for chunk in range(CHUNKS):
+        to_sibling(0, chunk).start()
+
+    v_row = vir_e[:, pl.ds(pl.multiple_of((r % tiles_virtual) * TILE, TILE), TILE)]
+    v_col = vir_e[:, pl.ds(pl.multiple_of((z % tiles_virtual) * TILE, TILE), TILE)]
+    row_energy = v_row - occ_e[r // tiles_virtual]
+    col_energy = v_col - occ_e[z // tiles_virtual]
+    denom[...] = jnp.broadcast_to(row_energy, (TILE, TILE)).T + col_energy
+
+    p_irr = occ_irr[r // tiles_virtual] ^ vir_irr[r % tiles_virtual]
+    q_irr = occ_irr[z // tiles_virtual] ^ vir_irr[z % tiles_virtual]
+    keep = jnp.where(p_irr == q_irr, 1.0, 0.0).astype(jnp.float32)
+
+    amp_copy.wait()
+    for tile in range(k_tiles):
+        number = z * k_tiles + tile
+        k_irr = occ_irr[number // tiles_virtual] ^ vir_irr[number % tiles_virtual]
+        same = jnp.where(p_irr == k_irr, 1.0, 0.0).astype(jnp.float32)
+        factor = jnp.full((TILE, TILE), same, jnp.float32).astype(jnp.bfloat16)
+        here = pl.ds(tile * TILE, TILE)
+        amp[:, here] = amp[:, here] * factor
+
+    def multiply(rel, m):
+        source = rows_of[rel] + m * shift
+        part[rel, m] = jnp.dot(amp[...], blocks[source], preferred_element_type=jnp.float32)
+
+    def z_unit(rel, m, s):
+        d = rows_of[rel] // 2
+        side = jnp.where(z > d, 1, 0)
+        rows = pl.ds(s * height, height)
+        unit = (rel * 2 + m) * SPLITS + s
+        copy = remote(
+            part.at[rel, m, rows],
+            incoming.at[side, rel, m, rows],
+            z_send.at[unit],
+            z_recv.at[side, unit],
+            (r, z + 1 - 2 * side),
+        )
+        upstream = jnp.where(z > d, nz - 1 - z, z)
+        return d, side, rows, unit, copy, upstream
+
+    def z_wait(side, rel, m, rows, unit):
+        ref = incoming.at[side, rel, m, rows]
+        remote(ref, ref, z_send.at[unit], z_recv.at[side, unit], (r, z)).wait_recv()
+
+    def z_begin(rel, m):
+        for s in range(SPLITS):
+            d, side, rows, unit, copy, upstream = z_unit(rel, m, s)
+
+            @pl.when(jnp.logical_and(z != d, upstream == 0))
+            def _():
+                copy.start()
+
+    def z_middle(rel, m):
+        for s in range(SPLITS):
+            d, side, rows, unit, copy, upstream = z_unit(rel, m, s)
+
+            @pl.when(jnp.logical_and(z != d, upstream > 0))
+            def _():
+                z_wait(side, rel, m, rows, unit)
+                part[rel, m, rows] = part[rel, m, rows] + incoming[side, rel, m, rows]
+                copy.start()
+
+    def z_end(rel, m):
+        for s in range(SPLITS):
+            d, side, rows, unit, copy, upstream = z_unit(rel, m, s)
+
+            @pl.when(z == d)
+            def _():
+                @pl.when(z > 0)
+                def _():
+                    z_wait(0, rel, m, rows, unit)
+                    part[rel, m, rows] = part[rel, m, rows] + incoming[0, rel, m, rows]
+
+                @pl.when(z < nz - 1)
+                def _():
+                    z_wait(1, rel, m, rows, unit)
+                    part[rel, m, rows] = part[rel, m, rows] + incoming[1, rel, m, rows]
+
+                side_of = core + m * shift
+                here = pl.ds(pl.multiple_of(side_of * COLS, COLS), COLS)
+                out_ref[rows, here] = part[rel, m, rows] * keep / denom[rows, here]
+
+            @pl.when(z != d)
+            def _():
+                copy.wait_send()
+
+    int_copy.wait()
+    multiply(0, 0)
+    z_begin(0, 0)
+    for chunk in range(CHUNKS):
+        sibling_arrival(0, chunk).wait_recv()
+    multiply(0, 1)
+    z_begin(0, 1)
+
+    for i, (cx, cy) in enumerate(zip(x_order, y_order)):
+        arrival(1, cx).wait_recv()
+        if cx < half:
+            forward(cx).start()
+        to_sibling(1, cx).start()
+        arrival(2, cy).wait_recv()
+        if cy >= half:
+            forward(cy).start()
+        to_sibling(2, cy).start()
+        if i == half - 1:
+            z_middle(0, 0)
+            z_middle(0, 1)
+    for rel in (1, 2):
+        multiply(rel, 0)
+        z_begin(rel, 0)
+    for rel in (1, 2):
+        for chunk in range(CHUNKS):
+            sibling_arrival(rel, chunk).wait_recv()
+        multiply(rel, 1)
+        z_begin(rel, 1)
+
+    for i in range(half):
+        for chunk in (i, i + half):
+            arrival(3, chunk).wait_recv()
+            to_sibling(3, chunk).start()
+        if i < half - 1:
+            for rel in (1, 2):
+                for m in (0, 1):
+                    z_middle(rel, m)
+    multiply(3, 0)
+    z_begin(3, 0)
+    for chunk in range(CHUNKS):
+        sibling_arrival(3, chunk).wait_recv()
+    multiply(3, 1)
+    z_begin(3, 1)
+    for m in (0, 1):
+        z_middle(3, m)
+    for rel in range(4):
+        for m in (0, 1):
+            z_end(rel, m)
+
+    for chunk in range(CHUNKS):
+        near(0, chunk).wait_send()
+        near(1, chunk).wait_send()
+        forward(chunk).wait_send()
+        for rel in range(4):
+            to_sibling(rel, chunk).wait_send()
+
+
+def fused(nz, amplitudes, integrals, occ_irrep, vir_irrep, occ_energy, vir_energy):
+    rows, depth = amplitudes.shape
+    smem = pl.BlockSpec(memory_space=pltpu.SMEM)
+    vmem = pl.BlockSpec(memory_space=pltpu.VMEM)
+    units = 8 * SPLITS
+    return pl.pallas_call(
+        functools.partial(cycle_kernel, nz),
+        out_shape=jax.ShapeDtypeStruct((rows, TILE), jnp.float32),
+        in_specs=[
+            pl.BlockSpec(memory_space=pl.ANY),
+            pl.BlockSpec(memory_space=pl.ANY),
+            smem,
+            smem,
+            smem,
+            vmem,
+        ],
+        out_specs=vmem,
+        scratch_shapes=[
+            pltpu.VMEM((8, depth, COLS), jnp.bfloat16),
+            pltpu.VMEM((rows, depth), jnp.bfloat16),
+            pltpu.VMEM((4, 2, rows, COLS), jnp.float32),
+            pltpu.VMEM((2, 4, 2, rows, COLS), jnp.float32),
+            pltpu.VMEM((rows, TILE), jnp.float32),
+            pltpu.SemaphoreType.DMA((2,)),
+            pltpu.SemaphoreType.DMA((2, CHUNKS)),
+            pltpu.SemaphoreType.DMA((3, CHUNKS)),
+            pltpu.SemaphoreType.DMA((CHUNKS,)),
+            pltpu.SemaphoreType.DMA((4, CHUNKS)),
+            pltpu.SemaphoreType.DMA((4, CHUNKS)),
+            pltpu.SemaphoreType.DMA((units,)),
+            pltpu.SemaphoreType.DMA((2, units)),
+        ],
+        compiler_params=pltpu.CompilerParams(
+            collective_id=0, has_side_effects=True, vmem_limit_bytes=32 << 20
+        ),
+    )(
+        amplitudes,
+        integrals,
+        occ_irrep,
+        vir_irrep,
+        occ_energy,
+        vir_energy.reshape(1, -1),
+    )
+
+
 def solution(mesh):
+    row, col = mesh.shape["row"], mesh.shape["col"]
+
+    def shards(amplitudes, integrals, occ_irrep, vir_irrep, occ_energy, vir_energy):
+        args = (amplitudes, integrals, occ_irrep, vir_irrep, occ_energy, vir_energy)
+        plain = (
+            (row, col) == (8, 4)
+            and amplitudes.shape[0] == TILE
+            and integrals.shape[1] == COLS
+            and vir_energy.shape[0] == TILE * vir_irrep.shape[0]
+        )
+        return fused(col, *args) if plain else general(*args)
+
     return jax.shard_map(
         shards,
         mesh=mesh,

time: 90.4 us -> 48.6 us (0.54); the launches traced: 88.6 us -> 48.4 us
  waiting for transfers between devices: 60.4 us -> 0 us
  Pallas kernels: 0 us -> 44.7 us
  between operations: 14.8 us -> 0.03 us
  other arithmetic: 11 us -> 0 us
  local copies, waits for them, and re-layouts: 0.1 us -> 3.72 us
  matrix products: 2.27 us -> 0 us
    pallas_call x0 -> x1, Pallas kernels: none -> 44.7 us  [fused(): pl.pallas_call(functools.partial(cycle_kernel, nz), out_shape=jax.ShapeDt...]
    all_gather x1 -> x0, waiting for transfers between devices: 32.2 us -> none  [shards(): piece = lax.all_gather(integrals, 'row', axis=1, tiled=True)]
    reduce_scatter x1 -> x0, waiting for transfers between devices: 27.5 us -> none  [shards(): lax.psum_scatter(partial_cycle, 'col', scatter_dimension=1, tiled=True)]
    reduce_sum x8 -> x0, other arithmetic: 6.58 us -> none  [lookup(): jnp.sum(jnp.where(hits, table[None, :], jnp.zeros_like(table)[None, :]),...]
    unnamed x8 -> x11, local copies, waits for them, and re-layouts: 0.1 us -> 2.98 us
    mul x1 -> x0, other arithmetic: 2.47 us -> none  [shards(): piece.reshape(k_tiles, tile_size, width) * keeper[:, None, :]]
    dot_general x1 -> x0, matrix products: 2.27 us -> none  [shards(): jnp.dot(masked_amp, masked_int, preferred_element_type=jnp.float32)]
    div x1 -> x0, other arithmetic: 1.76 us -> none  [shards(): return cycle / (row_energy[:, None] + col_energy[None, :])]
  transfers between devices with their start and end apart: 2 -> 0, of which waited for: 2 -> 0; matrix products, arithmetic and copies ran while one was open for 8% -> 0% of each run, Pallas kernels for 0% -> 0%
where the time goes in v1:
time: 48.6 us; the launch traced here: 48.4 us
  Pallas kernels  44.7 us (92%)
  local copies, waits for them, and re-layouts  3.72 us (8%)
    pallas_call x1, Pallas kernels, fused(): pl.pallas_call(functools.partial(cycle_kernel, nz), out_shape=jax.ShapeDt...  44.7 us
    unnamed x11, local copies, waits for them, and re-layouts  2.98 us

profile of v1, /device:TPU:6, one launch (start us, length us, event | category | flops | bytes accessed | tf_op | source)
XLA Modules:
  0.0 48.4 jit_solution(1038700371724714972)
XLA Ops:
  0.0 0.0 copy-start.3
  0.0 0.0 copy-start.4
  0.0 0.0 copy-start.2
  0.0 0.7 %reshape.3.vir_e = f32[1,1536]{1,0:T(1,128)S(1)} reshape(f32[1536]{0:T(1024)} %param.11) | data formatting | bytes 12288 | tf_op jit(solution)/shard_map/reshape | solution.py:371
  0.7 0.0 copy-done.3
  0.8 0.0 copy-done.4
  0.8 0.0 copy-done.2
  0.8 0.0 copy-start
  0.8 1.2 %copy-done = bf16[256,2048]{1,0:T(8,128)(2,1)S(1)} copy-done((bf16[256,2048]{1,0:T(8,128)(2,1)S(1)}, bf16[256,2048]{1,0:T(8,128)(2,1)}, u32[]{:S(2)}) %copy-start) | copy-done | bytes 1048600
  2.0 0.0 copy-start.1
  2.0 1.0 %copy-done.1 = bf16[2048,128]{1,0:T(8,128)(2,1)S(1)} copy-done((bf16[2048,128]{1,0:T(8,128)(2,1)S(1)}, bf16[2048,128]{1,0:T(8,128)(2,1)}, u32[]{:S(2)}) %copy-start.1) | copy-done | bytes 524312
  3.0 44.7 %shard_map.64 = f32[256,256]{1,0:T(8,128)S(1)} custom-call(bf16[256,2048]{1,0:T(8,128)(2,1)S(1)} %copy-done, bf16[2048,128]{1,0:T(8,128)(2,1)S(1)} %copy-done.1, s32[200]{0:T(256)S(1)} %copy-done.2, s32[6]{0:T(128)S(1)} %copy-done.4, f32[200]{0:T(256)S(1)} %copy-done.3, f32[1,1536]{1,0:T(1,128)S(1)} %reshape.3.vir_e), custom_call_target="tpu_custom_call" | custom-call | tf_op jit(solution)/shard_map/pallas_call | solution.py:335
  47.7 0.7 %copy.8 = f32[256,256]{1,0:T(8,128)} copy(f32[256,256]{1,0:T(8,128)S(1)} %shard_map.64) | data formatting | bytes 524288
Async XLA Ops:
  0.0 0.8 %copy-start.3 = (f32[200]{0:T(256)S(1)}, f32[200]{0:T(256)}, u32[]{:S(2)}) copy-start(f32[200]{0:T(256)} %occ_e.1) | copy-start | bytes 2404
  0.0 0.8 %copy-start.4 = (s32[6]{0:T(128)S(1)}, s32[6]{0:T(128)}, u32[]{:S(2)}) copy-start(s32[6]{0:T(128)} %vir_irr.1) | copy-start | bytes 76
  0.0 0.8 %copy-start.2 = (s32[200]{0:T(256)S(1)}, s32[200]{0:T(256)}, u32[]{:S(2)}) copy-start(s32[200]{0:T(256)} %occ_irr.1) | copy-start | bytes 2404
  0.8 1.2 %copy-start = (bf16[256,2048]{1,0:T(8,128)(2,1)S(1)}, bf16[256,2048]{1,0:T(8,128)(2,1)}, u32[]{:S(2)}) copy-start(bf16[256,2048]{1,0:T(8,128)(2,1)} %amp_hbm.1) | copy-start | bytes 3145732
  2.0 1.0 %copy-start.1 = (bf16[2048,128]{1,0:T(8,128)(2,1)S(1)}, bf16[2048,128]{1,0:T(8,128)(2,1)}, u32[]{:S(2)}) copy-start(bf16[2048,128]{1,0:T(8,128)(2,1)} %int_hbm.1) | copy-start | bytes 1572868

commit v2 on v0

--- a/solution.py
+++ b/solution.py
@@ -1,9 +1,14 @@
+import functools
+
 import jax
 import jax.numpy as jnp
 from jax import lax
+from jax.experimental import pallas as pl
+from jax.experimental.pallas import tpu as pltpu
 from jax.sharding import PartitionSpec as P
 
 TILE = 256
+MESH = pl.DeviceIdType.MESH
 
 
 def lookup(table, index):
@@ -18,7 +23,7 @@
     )
 
 
-def shards(amplitudes, integrals, occ_irrep, vir_irrep, occ_energy, vir_energy):
+def general(amplitudes, integrals, occ_irrep, vir_irrep, occ_energy, vir_energy):
     tile_size = TILE
     tiles_virtual = vir_irrep.shape[0]
     virtual_count = vir_energy.shape[0]
@@ -60,7 +65,325 @@
     return cycle / (row_energy[:, None] + col_energy[None, :])
 
 
+CHUNKS = 4
+COLS = 128
+SLOTS = 8
+TOP = 32767.0
+
+
+def select_tiles(k_irr, irrep, slots):
+    tiles = len(k_irr)
+    found = [jnp.int32(tiles)] * slots
+    count = jnp.int32(0)
+    for tile in range(tiles):
+        hit = k_irr[tile] == irrep
+        found = [
+            jnp.where(jnp.logical_and(hit, count == s), tile, found[s]) for s in range(slots)
+        ]
+        count = count + jnp.where(hit, 1, 0)
+    return found
+
+
+def cycle_kernel(
+    nz,
+    slots,
+    amp_hbm,
+    int_hbm,
+    occ_irr,
+    vir_irr,
+    occ_e,
+    vir_e,
+    out_ref,
+    mine,
+    blocks,
+    amp,
+    own,
+    codes,
+    scales,
+    in_codes,
+    in_scales,
+    denom,
+    int_sem,
+    amp_sem,
+    near_send,
+    near_recv,
+    fwd_send,
+    sib_send,
+    sib_recv,
+    z_send,
+    z_recv,
+):
+    r = lax.axis_index("row")
+    z = lax.axis_index("col")
+    core = r % 2
+    x = (r // 2) % 2
+    y = r // 4
+    xr = r + 2 - 4 * x
+    yr = r + 4 - 8 * y
+    dr = xr + yr - r
+    shift = 1 - 2 * core
+    sr = r + shift
+    rows_of = (r, xr, yr, dr)
+    tiles_virtual = vir_irr.shape[0]
+    k_tiles = mine.shape[0]
+    dense = slots == k_tiles
+    step = slots * TILE // CHUNKS
+
+    def remote(src, dst, send_sem, recv_sem, target):
+        return pltpu.make_async_remote_copy(
+            src_ref=src,
+            dst_ref=dst,
+            send_sem=send_sem,
+            recv_sem=recv_sem,
+            device_id=target,
+            device_id_type=MESH,
+        )
+
+    int_copies = []
+    for tile in range(k_tiles):
+        here = pl.ds(tile * TILE, TILE)
+        copy = pltpu.make_async_copy(int_hbm.at[here], mine.at[tile], int_sem.at[tile])
+        copy.start()
+        int_copies.append(copy)
+    amp_copies = []
+    for tile in range(k_tiles):
+        here = pl.ds(tile * TILE, TILE)
+        copy = pltpu.make_async_copy(amp_hbm.at[:, here], amp.at[tile], amp_sem.at[tile])
+        copy.start()
+        amp_copies.append(copy)
+
+    barrier = pltpu.get_barrier_semaphore()
+    for target in (xr, yr, sr):
+        pl.semaphore_signal(barrier, inc=1, device_id=(target, z), device_id_type=MESH)
+    for k in range(1, nz):
+        pl.semaphore_signal(barrier, inc=1, device_id=(r, (z + k) % nz), device_id_type=MESH)
+
+    def irrep(number):
+        return occ_irr[number // tiles_virtual] ^ vir_irr[number % tiles_virtual]
+
+    p_irr = irrep(r)
+    q_irr = irrep(z)
+    k_irr = [irrep(z * k_tiles + tile) for tile in range(k_tiles)]
+    keep = jnp.where(p_irr == q_irr, 1.0, 0.0).astype(jnp.float32)
+    if dense:
+        chosen = [list(range(k_tiles))] * 4
+    else:
+        chosen = [select_tiles(k_irr, irrep(source // 2), slots) for source in rows_of]
+
+    for copy in int_copies:
+        copy.wait()
+    for s in range(slots):
+        tile = chosen[0][s] if dense else jnp.minimum(chosen[0][s], k_tiles - 1)
+        blocks[r, pl.ds(s * TILE, TILE)] = mine[tile]
+
+    pl.semaphore_wait(barrier, 3 + nz - 1)
+
+    half = CHUNKS // 2
+    x_order = list(range(CHUNKS))
+    y_order = x_order[half:] + x_order[:half]
+
+    def piece(source, chunk):
+        return blocks.at[source, pl.ds(chunk * step, step)]
+
+    def near(axis, chunk):
+        ref = piece(r, chunk)
+        return remote(
+            ref, ref, near_send.at[axis, chunk], near_recv.at[axis, chunk], ((xr, yr)[axis], z)
+        )
+
+    def arrival(rel, chunk):
+        ref = piece(rows_of[rel], chunk)
+        return remote(ref, ref, near_send.at[0, chunk], near_recv.at[rel - 1, chunk], (xr, z))
+
+    def forward(chunk):
+        source, target = (xr, yr) if chunk < half else (yr, xr)
+        ref = piece(source, chunk)
+        return remote(ref, ref, fwd_send.at[chunk], near_recv.at[2, chunk], (target, z))
+
+    def to_sibling(rel, chunk):
+        ref = piece(rows_of[rel], chunk)
+        return remote(ref, ref, sib_send.at[rel, chunk], sib_recv.at[rel, chunk], (sr, z))
+
+    def sibling_arrival(rel, chunk):
+        ref = piece(rows_of[rel] + shift, chunk)
+        return remote(ref, ref, sib_send.at[rel, chunk], sib_recv.at[rel, chunk], (sr, z))
+
+    for cx, cy in zip(x_order, y_order):
+        near(0, cx).start()
+        near(1, cy).start()
+    for chunk in range(CHUNKS):
+        to_sibling(0, chunk).start()
+
+    amp[k_tiles] = jnp.zeros((TILE, TILE), jnp.bfloat16)
+    for tile in range(k_tiles):
+        amp_copies[tile].wait()
+        same = jnp.where(p_irr == k_irr[tile], 1.0, 0.0).astype(jnp.float32)
+        amp[tile] = amp[tile] * jnp.full((TILE, TILE), same, jnp.float32).astype(jnp.bfloat16)
+
+    def code_send(rel, m, d):
+        return (
+            remote(
+                codes.at[rel, m],
+                in_codes.at[z, m],
+                z_send.at[0, rel, m],
+                z_recv.at[0, z, m],
+                (r, d),
+            ),
+            remote(
+                scales.at[rel, m],
+                in_scales.at[z, m],
+                z_send.at[1, rel, m],
+                z_recv.at[1, z, m],
+                (r, d),
+            ),
+        )
+
+    def multiply(rel, m):
+        source = rows_of[rel]
+        d = source // 2
+        left = jnp.concatenate([amp[tile] for tile in chosen[rel]], axis=1)
+        product = jnp.dot(
+            left, blocks[source + m * shift], preferred_element_type=jnp.float32
+        )
+
+        @pl.when(z == d)
+        def _():
+            own[m] = product
+
+        @pl.when(z != d)
+        def _():
+            parts = product.reshape(TILE // 8, 8, COLS)
+            most = jnp.maximum(jnp.max(jnp.abs(parts), axis=0), 1e-30)
+            scales[rel, m] = most * (1.0 / TOP)
+            scaled = jnp.floor(parts * (TOP / most)[None] + 0.5)
+            whole = jnp.clip(scaled, -TOP, TOP).astype(jnp.int32)
+            codes[rel, m] = whole.reshape(TILE, COLS).astype(jnp.int16)
+            for copy in code_send(rel, m, d):
+                copy.start()
+
+    multiply(0, 0)
+    for chunk in range(CHUNKS):
+        sibling_arrival(0, chunk).wait_recv()
+    multiply(0, 1)
+
+    for cx, cy in zip(x_order, y_order):
+        arrival(1, cx).wait_recv()
+        if cx < half:
+            forward(cx).start()
+        to_sibling(1, cx).start()
+        arrival(2, cy).wait_recv()
+        if cy >= half:
+            forward(cy).start()
+        to_sibling(2, cy).start()
+    for rel in (1, 2):
+        multiply(rel, 0)
+    for rel in (1, 2):
+        for chunk in range(CHUNKS):
+            sibling_arrival(rel, chunk).wait_recv()
+        multiply(rel, 1)
+
+    v_row = vir_e[:, pl.ds(pl.multiple_of((r % tiles_virtual) * TILE, TILE), TILE)]
+    v_col = vir_e[:, pl.ds(pl.multiple_of((z % tiles_virtual) * TILE, TILE), TILE)]
+    row_energy = v_row - occ_e[r // tiles_virtual]
+    col_energy = v_col - occ_e[z // tiles_virtual]
+    denom[...] = jnp.broadcast_to(row_energy, (TILE, TILE)).T + col_energy
+
+    for i in range(half):
+        for chunk in (i, i + half):
+            arrival(3, chunk).wait_recv()
+            to_sibling(3, chunk).start()
+    multiply(3, 0)
+    for chunk in range(CHUNKS):
+        sibling_arrival(3, chunk).wait_recv()
+    multiply(3, 1)
+
+    for m in (0, 1):
+        total = own[m]
+        for k in range(1, nz):
+            source = (z + k) % nz
+            code_ref = in_codes.at[source, m]
+            scale_ref = in_scales.at[source, m]
+            target = (r, source)
+            remote(
+                code_ref, code_ref, z_send.at[0, 0, m], z_recv.at[0, source, m], target
+            ).wait_recv()
+            remote(
+                scale_ref, scale_ref, z_send.at[1, 0, m], z_recv.at[1, source, m], target
+            ).wait_recv()
+            values = in_codes[source, m].astype(jnp.int32).astype(jnp.float32)
+            values = values.reshape(TILE // 8, 8, COLS) * in_scales[source, m][None]
+            total = total + values.reshape(TILE, COLS)
+        here = pl.ds(pl.multiple_of((core + m * shift) * COLS, COLS), COLS)
+        out_ref[:, here] = total * keep / denom[:, here]
+
+    for rel in range(4):
+        d = rows_of[rel] // 2
+
+        @pl.when(z != d)
+        def _():
+            for m in (0, 1):
+                for copy in code_send(rel, m, d):
+                    copy.wait_send()
+
+    for chunk in range(CHUNKS):
+        near(0, chunk).wait_send()
+        near(1, chunk).wait_send()
+        forward(chunk).wait_send()
+        for rel in range(4):
+            to_sibling(rel, chunk).wait_send()
+
+
+def fused(nz, slots, amplitudes, integrals, occ_irrep, vir_irrep, occ_energy, vir_energy):
+    rows, depth = amplitudes.shape
+    k_tiles = depth // TILE
+    smem = pl.BlockSpec(memory_space=pltpu.SMEM)
+    vmem = pl.BlockSpec(memory_space=pltpu.VMEM)
+    hbm = pl.BlockSpec(memory_space=pltpu.HBM)
+    dma = pltpu.SemaphoreType.DMA
+    return pl.pallas_call(
+        functools.partial(cycle_kernel, nz, slots),
+        out_shape=jax.ShapeDtypeStruct((rows, TILE), jnp.float32),
+        in_specs=[hbm, hbm, smem, smem, smem, vmem],
+        out_specs=vmem,
+        scratch_shapes=[
+            pltpu.VMEM((k_tiles, TILE, COLS), jnp.bfloat16),
+            pltpu.VMEM((8, slots * TILE, COLS), jnp.bfloat16),
+            pltpu.VMEM((k_tiles + 1, rows, TILE), jnp.bfloat16),
+            pltpu.VMEM((2, rows, COLS), jnp.float32),
+            pltpu.VMEM((4, 2, rows, COLS), jnp.int16),
+            pltpu.VMEM((4, 2, 8, COLS), jnp.float32),
+            pltpu.VMEM((nz, 2, rows, COLS), jnp.int16),
+            pltpu.VMEM((nz, 2, 8, COLS), jnp.float32),
+            pltpu.VMEM((rows, TILE), jnp.float32),
+            dma((k_tiles,)),
+            dma((k_tiles,)),
+            dma((2, CHUNKS)),
+            dma((3, CHUNKS)),
+            dma((CHUNKS,)),
+            dma((4, CHUNKS)),
+            dma((4, CHUNKS)),
+            dma((2, 4, 2)),
+            dma((2, nz, 2)),
+        ],
+        compiler_params=pltpu.CompilerParams(
+            collective_id=slots, has_side_effects=True, vmem_limit_bytes=48 << 20
+        ),
+    )(amplitudes, integrals, occ_irrep, vir_irrep, occ_energy, vir_energy.reshape(1, -1))
+
+
 def solution(mesh):
+    row, col = mesh.shape["row"], mesh.shape["col"]
+
+    def shards(amplitudes, integrals, occ_irrep, vir_irrep, occ_energy, vir_energy):
+        args = (amplitudes, integrals, occ_irrep, vir_irrep, occ_energy, vir_energy)
+        plain = (
+            (row, col) == (8, 4)
+            and amplitudes.shape[0] == TILE
+            and integrals.shape[1] == COLS
+            and vir_energy.shape[0] == TILE * vir_irrep.shape[0]
+        )
+        return fused(col, SLOTS, *args) if plain else general(*args)
+
     return jax.shard_map(
         shards,
         mesh=mesh,

time: 90.4 us -> 38.4 us (0.42); the launches traced: 88.6 us -> 38.2 us
  waiting for transfers between devices: 60.4 us -> 0 us
  Pallas kernels: 0 us -> 34.4 us
  between operations: 14.8 us -> 0.03 us
  other arithmetic: 11 us -> 0 us
  local copies, waits for them, and re-layouts: 0.1 us -> 3.72 us
  matrix products: 2.27 us -> 0 us
    pallas_call x0 -> x1, Pallas kernels: none -> 34.4 us  [fused(): pl.pallas_call(functools.partial(cycle_kernel, nz, slots), out_shape=jax....]
    all_gather x1 -> x0, waiting for transfers between devices: 32.2 us -> none  [shards(): piece = lax.all_gather(integrals, 'row', axis=1, tiled=True)]
    reduce_scatter x1 -> x0, waiting for transfers between devices: 27.5 us -> none  [shards(): lax.psum_scatter(partial_cycle, 'col', scatter_dimension=1, tiled=True)]
    reduce_sum x8 -> x0, other arithmetic: 6.58 us -> none  [lookup(): jnp.sum(jnp.where(hits, table[None, :], jnp.zeros_like(table)[None, :]),...]
    unnamed x8 -> x11, local copies, waits for them, and re-layouts: 0.1 us -> 2.98 us
    mul x1 -> x0, other arithmetic: 2.47 us -> none  [shards(): piece.reshape(k_tiles, tile_size, width) * keeper[:, None, :]]
    dot_general x1 -> x0, matrix products: 2.27 us -> none  [shards(): jnp.dot(masked_amp, masked_int, preferred_element_type=jnp.float32)]
    div x1 -> x0, other arithmetic: 1.76 us -> none  [shards(): return cycle / (row_energy[:, None] + col_energy[None, :])]
  transfers between devices with their start and end apart: 2 -> 0, of which waited for: 2 -> 0; matrix products, arithmetic and copies ran while one was open for 8% -> 0% of each run, Pallas kernels for 0% -> 0%
where the time goes in v2:
time: 38.4 us; the launch traced here: 38.2 us
  Pallas kernels  34.4 us (90%)
  local copies, waits for them, and re-layouts  3.72 us (10%)
    pallas_call x1, Pallas kernels, fused(): pl.pallas_call(functools.partial(cycle_kernel, nz, slots), out_shape=jax....  34.4 us
    unnamed x11, local copies, waits for them, and re-layouts  2.98 us

profile of v2, /device:TPU:6, one launch (start us, length us, event | category | flops | bytes accessed | tf_op | source)
XLA Modules:
  0.0 38.2 jit_solution(13304537062048167880)
XLA Ops:
  0.0 0.0 copy-start.3
  0.0 0.0 copy-start.4
  0.0 0.0 copy-start.2
  0.0 0.7 %reshape.3.vir_e = f32[1,1536]{1,0:T(1,128)S(1)} reshape(f32[1536]{0:T(1024)} %param.11) | data formatting | bytes 12288 | tf_op jit(solution)/shard_map/reshape | solution.py:371
  0.7 0.0 copy-done.3
  0.8 0.0 copy-done.4
  0.8 0.0 copy-done.2
  0.8 0.0 copy-start
  0.8 1.2 %copy-done = bf16[256,2048]{1,0:T(8,128)(2,1)S(1)} copy-done((bf16[256,2048]{1,0:T(8,128)(2,1)S(1)}, bf16[256,2048]{1,0:T(8,128)(2,1)}, u32[]{:S(2)}) %copy-start) | copy-done | bytes 1048600
  2.0 0.0 copy-start.1
  2.0 1.0 %copy-done.1 = bf16[2048,128]{1,0:T(8,128)(2,1)S(1)} copy-done((bf16[2048,128]{1,0:T(8,128)(2,1)S(1)}, bf16[2048,128]{1,0:T(8,128)(2,1)}, u32[]{:S(2)}) %copy-start.1) | copy-done | bytes 524312
  3.0 34.4 %shard_map.64 = f32[256,256]{1,0:T(8,128)S(1)} custom-call(bf16[256,2048]{1,0:T(8,128)(2,1)S(1)} %copy-done, bf16[2048,128]{1,0:T(8,128)(2,1)S(1)} %copy-done.1, s32[200]{0:T(256)S(1)} %copy-done.2, s32[6]{0:T(128)S(1)} %copy-done.4, f32[200]{0:T(256)S(1)} %copy-done.3, f32[1,1536]{1,0:T(1,128)S(1)} %reshape.3.vir_e), custom_call_target="tpu_custom_call" | custom-call | tf_op jit(solution)/shard_map/pallas_call | solution.py:343
  37.4 0.7 %copy.8 = f32[256,256]{1,0:T(8,128)} copy(f32[256,256]{1,0:T(8,128)S(1)} %shard_map.64) | data formatting | bytes 524288
Async XLA Ops:
  0.0 0.8 %copy-start.3 = (f32[200]{0:T(256)S(1)}, f32[200]{0:T(256)}, u32[]{:S(2)}) copy-start(f32[200]{0:T(256)} %occ_e.1) | copy-start | bytes 2404
  0.0 0.8 %copy-start.4 = (s32[6]{0:T(128)S(1)}, s32[6]{0:T(128)}, u32[]{:S(2)}) copy-start(s32[6]{0:T(128)} %vir_irr.1) | copy-start | bytes 76
  0.0 0.8 %copy-start.2 = (s32[200]{0:T(256)S(1)}, s32[200]{0:T(256)}, u32[]{:S(2)}) copy-start(s32[200]{0:T(256)} %occ_irr.1) | copy-start | bytes 2404
  0.8 1.2 %copy-start = (bf16[256,2048]{1,0:T(8,128)(2,1)S(1)}, bf16[256,2048]{1,0:T(8,128)(2,1)}, u32[]{:S(2)}) copy-start(bf16[256,2048]{1,0:T(8,128)(2,1)} %amp_hbm.1) | copy-start | bytes 3145732
  2.0 1.0 %copy-start.1 = (bf16[2048,128]{1,0:T(8,128)(2,1)S(1)}, bf16[2048,128]{1,0:T(8,128)(2,1)}, u32[]{:S(2)}) copy-start(bf16[2048,128]{1,0:T(8,128)(2,1)} %int_hbm.1) | copy-start | bytes 1572868
